TPU v7x, 32 devices: a whole 2x2x4 slice. The times are simulated.
32 devices in a mesh: fsdp: 4 (over z), dp: 2 (over y), tensor: 4 (over x, core).
Axes of the slice: x: 2, y: 2, z: 4, core: 2. Of those that a mesh axis runs over, the one named last changes fastest.
Arguments:
- tokens: bfloat16 [2048, 7168], P(('fsdp', 'dp')), may hold values from -6 to 6
- panels: bfloat16 [112, 4, 128, 128], P('tensor', None, 'fsdp'), may hold values from -0.25 to 0.25
- block_rows: int32 [112, 4], P('tensor'), may hold values from 0 to 55, as said below
- low_in: bfloat16 [7168, 512], P('tensor'), may hold values from -0.0625 to 0.0625
- low_out: bfloat16 [112, 4, 128, 128], P('tensor'), may hold values from -0.25 to 0.25
- cotangent: bfloat16 [2048, 14336], P(('fsdp', 'dp'), 'tensor'), may hold values from -0.125 to 0.125
Outputs:
- activated: bfloat16 [2048, 14336], P(('fsdp', 'dp'), 'tensor')
- panel_grad: float32 [112, 4, 128, 128], P('tensor', None, 'fsdp')
Inputs may be any that keep to these rules, and one draw needn't show every extreme that they name: `block_rows`: each column block c names 4 distinct row blocks, the first of them c modulo 56.
All inputs are finite; a program needn't handle non-finite values.
Results may differ from a plain program's by a relative error of at most 0.0039.
Values may be sent and summed in bfloat16 or wider, within the bound.
A program may use at most 128 MiB of HBM per device.

v0:
```python
import jax
import jax.numpy as jnp
from jax import lax
from jax.sharding import PartitionSpec as P


def activate(values):
    return jax.nn.gelu(values, approximate=True)


def on_device(tokens, panels, block_rows, low_in, low_out, cotangent):
    tok_count = tokens.shape[0]
    local_cols, per_column, part_rows, blk_width = panels.shape
    feature_blocks = tokens.shape[1] // blk_width
    tiled_rows = tokens.reshape(tok_count, feature_blocks, blk_width)
    picked = jnp.take(tiled_rows, block_rows.reshape(-1), axis=1)
    picked = picked.reshape(tok_count, local_cols, per_column, blk_width)
    slice_width = low_in.shape[0]
    own_slice = lax.dynamic_slice_in_dim(
        tokens, lax.axis_index("tensor") * slice_width, slice_width, 1
    )
    partial_low = jnp.dot(own_slice, low_in, preferred_element_type=jnp.float32)
    latent = lax.psum(partial_low, "tensor").astype(jnp.bfloat16)
    latent_tiles = latent.reshape(tok_count, low_out.shape[1], blk_width)
    low_part = jnp.einsum(
        "tjr,cjro->tco", latent_tiles, low_out, preferred_element_type=jnp.float32
    )
    panels_all = lax.all_gather(panels, "fsdp", axis=2, tiled=True)
    pre = low_part + jnp.einsum(
        "tckr,ckro->tco", picked, panels_all, preferred_element_type=jnp.float32
    )
    result, pullback = jax.vjp(activate, pre)
    activated = result.astype(jnp.bfloat16).reshape(tok_count, local_cols * blk_width)
    slope_in = cotangent.reshape(tok_count, local_cols, blk_width).astype(jnp.float32)
    slope = pullback(slope_in)[0].astype(jnp.bfloat16)
    local_grad = jnp.einsum("tckr,tco->ckro", picked, slope, preferred_element_type=jnp.float32)
    grad_shard = lax.psum_scatter(local_grad, "fsdp", scatter_dimension=2, tiled=True)
    panel_grad = lax.psum(grad_shard, "dp")
    return (activated, panel_grad)


def solution(mesh):
    in_specs = (
        P(("fsdp", "dp"), None),
        P("tensor", None, "fsdp", None),
        P("tensor", None),
        P("tensor", None),
        P("tensor", None, None, None),
        P(("fsdp", "dp"), "tensor"),
    )
    out_specs = (P(("fsdp", "dp"), "tensor"), P("tensor", None, "fsdp", None))
    return jax.shard_map(
        on_device, mesh=mesh, in_specs=in_specs, out_specs=out_specs, check_vma=False
    )
```

profile of v0, /device:TPU:0, one launch (start us, length us, event | category | flops | bytes accessed | tf_op | source)
XLA Modules:
  0.0 302.3 jit_solution(1937555755613458812)
XLA Ops:
  7.2 0.0 all-gather.2.cloned.1.call-start
  7.2 0.7 all-gather.2.cloned.1.call-update
  7.9 0.0 reduce-scatter.2.cloned.1.call-start
  8.0 5.9 %copy.29 = bf16[256,7168]{0,1:T(8,128)(2,1)} copy(bf16[256,7168]{1,0:T(8,128)(2,1)} %param.6) | data formatting | bytes 7340032 | tf_op args[0]
  13.9 5.9 %copy.31 = bf16[256,56,128]{2,0,1:T(8,128)(2,1)} copy(bf16[256,56,128]{0,2,1:T(8,128)(2,1)} %bitcast.41) | data formatting | bytes 7340032 | tf_op jit(solution)/shard_map/reshape | solution.py:15
  19.8 0.1 copy.30
  19.9 0.1 reshape.58
  20.0 8.7 %gather_fusion = bf16[112,256,128]{2,1,0:T(8,128)(2,1)} fusion(bf16[256,56,128]{2,0,1:T(8,128)(2,1)} %copy.31, s32[1024]{0:T(1024)S(1)} %pad_clamp_fusion), kind=kCustom, calls=%fused_computation | custom fusion | bytes 14680512 | tf_op jit(solution)/shard_map/jit(_take)/gather | solution.py:16
  28.7 10.4 %copy.32 = bf16[256,28,4,128]{0,3,2,1:T(8,128)(2,1)} copy(bf16[256,28,4,128]{3,0,2,1:T(8,128)(2,1)} %bitcast.40) | data formatting | bytes 14680064 | tf_op jit(solution)/shard_map/jit(_take)/gather | solution.py:16
  39.1 0.1 copy.28
  39.2 1.8 fusion.18
  41.1 4.0 %copy.34 = f32[256,3584]{0,1:T(8,128)} copy(bf16[256,3584]{1,0:T(8,128)(2,1)} %param.11) | data formatting | bytes 5505024 | tf_op jit(solution)/shard_map/convert_element_type | solution.py:34
  45.1 19.1 %all-reduce.4 = bf16[256,512]{1,0:T(8,128)(2,1)S(1)} all-reduce(f32[256,512]{1,0:T(8,128)S(1)} %fusion.18), channel_id=1, replica_groups=mesh['fsdp'=4,'dp'=2,'tensor'=4] {'tensor'}, use_global_device_ids=true, to_apply=%region_0.1 | all-reduce | flops 131072 | bytes 786432 | tf_op jit(solution)/shard_map/psum | solution.py:23
  64.2 20.3 %all-gather.2.cloned.1.call-done = bf16[28,4,128,128]{3,2,1,0:T(8,128)(2,1)} async-done(((bf16[28,4,32,128]{3,2,1,0:T(8,128)(2,1)}), bf16[28,4,128,128]{3,2,1,0:T(8,128)(2,1)}) %all-gather.2.cloned.1.call-update) | async-done | bytes 3670032 | tf_op jit(solution)/shard_map/all_gather | solution.py:28
  84.5 7.8 %fusion.1 = f32[28,256,128,1]{1,2,3,0:T(8,128)} fusion(bf16[28,4,128,128]{3,2,1,0:T(8,128)(2,1)} %all-gather.2.cloned.1.call-done, bf16[256,28,4,128]{0,3,2,1:T(8,128)(2,1)} %copy.32, pred[28,4]{1,0:T(8,128)(4,1)S(1)} %copy.28), kind=kOutput, calls=%fused_computation.3 | convolution fusion | flops 943194112 | bytes 14680176 | tf_op jit(solution)/shard_map/tckr,ckro->tco/dot_general | solution.py:29
  92.2 5.9 %multiply_convert_fusion = (bf16[256,28,128]{0,2,1:T(8,128)(2,1)}, f32[256,28,128]{0,2,1:T(8,128)S(1)}) fusion(f32[28,256,128,1]{1,2,3,0:T(8,128)} %fusion.1, bf16[28,4,128,128]{3,2,1,0:T(8,128)(2,1)S(1)} %copy-done.3, bf16[256,512]{1,0:T(8,128)(2,1)S(1)} %all-reduce.4), kind=kOutput, calls=%fused_computation.14 | convolution fusion | flops 948699136 | bytes 13107200 | tf_op jit(solution)/shard_map/tjr,cjro->tco/dot_general | solution.py:25
  98.1 8.1 %fusion = f32[28,4,128,128]{3,2,1,0:T(8,128)} fusion(bf16[256,28,4,128]{0,3,2,1:T(8,128)(2,1)} %copy.32, pred[28,4]{1,0:T(8,128)(4,1)S(1)} %copy.28, f32[256,28,128]{0,2,1:T(8,128)S(1)} %get-tuple-element.9, f32[256,28,128]{0,2,1:T(8,128)S(1)} %bitcast.42), kind=kOutput, calls=%fused_computation.2 | convolution fusion | flops 961544192 | bytes 22020208 | tf_op jit(solution)/shard_map/tckr,tco->ckro/dot_general | solution.py:36
  106.2 0.0 reduce-scatter.2.cloned.1.call-update
  106.2 0.0 all-reduce.3.cloned.1.call-start
  106.3 126.5 %reduce-scatter.2.cloned.1.call-done = f32[28,4,32,128]{3,2,1,0:T(8,128)} async-done(((f32[28,4,128,128]{3,2,1,0:T(8,128)}), f32[28,4,32,128]{3,2,1,0:T(8,128)}) %reduce-scatter.2.cloned.1.call-update) | async-done | bytes 1835024 | tf_op jit(solution)/shard_map/reduce_scatter | solution.py:37
  232.7 0.0 all-reduce.3.cloned.1.call-update
  232.8 3.8 %copy.36 = bf16[256,3584]{1,0:T(8,128)(2,1)} copy(bf16[256,3584]{0,1:T(8,128)(2,1)} %bitcast.43) | data formatting | bytes 3670016
  236.6 56.2 %all-reduce.3.cloned.1.call-done = f32[28,4,32,128]{3,2,1,0:T(8,128)} async-done(((f32[28,4,32,128]{3,2,1,0:T(8,128)}), f32[28,4,32,128]{3,2,1,0:T(8,128)}) %all-reduce.3.cloned.1.call-update) | async-done | bytes 1835024 | tf_op jit(solution)/shard_map/psum | solution.py:38
  292.8 3.0 copy.54
  (11 shorter events, 0.0 us)
Async XLA Ops:
  7.2 32.1 %copy-start = (bf16[1792,512]{1,0:T(8,128)(2,1)S(1)}, bf16[1792,512]{1,0:T(8,128)(2,1)}, u32[]{:S(2)}) copy-start(bf16[1792,512]{1,0:T(8,128)(2,1)} %param.9) | copy-start | bytes 5505028
  7.2 77.3 %all-gather.2.cloned.1.call-start = ((), (), s32[]{:S(2)}) async-start(), calls=%async_computation.1 | async-start | bytes 4587520 | tf_op jit(solution)/shard_map/all_gather | solution.py:28
  7.9 224.8 %reduce-scatter.2.cloned.1.call-start = ((), (), s32[]{:S(2)}) async-start(), calls=%async_computation.2 | async-start | bytes 9175040 | tf_op jit(solution)/shard_map/reduce_scatter | solution.py:37
  13.9 5.9 %copy-start.2 = (s32[28,4]{0,1:T(4,128)S(1)}, s32[28,4]{0,1:T(4,128)}, u32[]{:S(2)}) copy-start(s32[28,4]{0,1:T(4,128)} %param.8) | copy-start | bytes 1348
  84.4 7.8 %copy-start.3 = (bf16[28,4,128,128]{3,2,1,0:T(8,128)(2,1)S(1)}, bf16[28,4,128,128]{3,2,1,0:T(8,128)(2,1)}, u32[]{:S(2)}) copy-start(bf16[28,4,128,128]{3,2,1,0:T(8,128)(2,1)} %param.10) | copy-start | bytes 11010052
  92.2 5.9 %copy-start.1 = (f32[256,3584]{0,1:T(8,128)S(1)}, f32[256,3584]{0,1:T(8,128)}, u32[]{:S(2)}) copy-start(f32[256,3584]{0,1:T(8,128)} %copy.34) | copy-start | bytes 11010052
  106.2 186.6 %all-reduce.3.cloned.1.call-start = ((), (), s32[]{:S(2)}) async-start(), calls=%async_computation.3 | async-start | bytes 3670016 | tf_op jit(solution)/shard_map/psum | solution.py:38
Sparse Core Ops, SparseCore 0:
  9.6 74.8 all-gather.1
  106.3 126.3 reduce-scatter.1
  235.0 57.6 all-reduce.2
where the time goes:
time: 303 us; the launch traced here: 302 us
  waiting for transfers between devices  204 us (67%)
  local copies, waits for them, and re-layouts  42 us (14%)
  matrix products  23.5 us (8%)
  blocking collectives  19.1 us (6%)
  between operations  13.8 us (5%)
    reduce_scatter x1, waiting for transfers between devices, on_device(): lax.psum_scatter(local_grad, 'fsdp', scatter_dimension=2, tiled=True)  126 us
    psum x1, waiting for transfers between devices, on_device(): panel_grad = lax.psum(grad_shard, 'dp')  56.2 us
    all_gather x1, waiting for transfers between devices, on_device(): panels_all = lax.all_gather(panels, 'fsdp', axis=2, tiled=True)  20.3 us
    psum x1, blocking collectives, on_device(): latent = lax.psum(partial_low, 'tensor').astype(jnp.bfloat16)  19.1 us
    gather x2, local copies, waits for them, and re-layouts, on_device(): picked = jnp.take(tiled_rows, block_rows.reshape(-1), axis=1)  19.1 us
    unnamed x12, local copies, waits for them, and re-layouts  12.8 us
    dot_general x1, matrix products, on_device(): jnp.einsum('tckr,tco->ckro', picked, slope, preferred_element_type=jnp.fl...  8.1 us
    dot_general x1, matrix products, on_device(): jnp.einsum('tckr,ckro->tco', picked, panels_all, preferred_element_type=j...  7.75 us
  transfers between devices with their start and end apart: 3, of which 3 were waited for; matrix products, arithmetic and copies ran while one was open for 14% of the time, Pallas kernels for 0%

commit v1 on v0

v1 whole, which is shorter than its diff:
```python
import functools
import math

import jax
import jax.numpy as jnp
from jax import lax
from jax.experimental import pallas as pl
from jax.experimental.pallas import tpu as pltpu
from jax.sharding import PartitionSpec as P

MESH = pl.DeviceIdType.MESH
GELU_SCALE = math.sqrt(2.0 / math.pi)
GELU_CUBIC = 0.044715
AHEAD = 2


def kernel(
    nz, ny, nt, nc,
    tokens_hbm, panels_hbm, rows_ref, low_in_hbm, low_out_hbm, cot_hbm,
    act_ref, grad_ref,
    tok, lin, lout, cot, pan, own, sbuf, rbuf, ysend, yrecv, lpart, lrecv, lat,
    local_sem, tok_sem, ag_send, ag_recv, rs_send, rs_recv, y_send, y_recv,
    l1_send, l1_recv, l2_send, l2_recv,
):
    z, y, t = lax.axis_index("fsdp"), lax.axis_index("dp"), lax.axis_index("tensor")
    cols, per, rows, blk = panels_hbm.shape
    chunks = cols // nc
    f32 = jnp.float32

    in_copies = [
        pltpu.make_async_copy(src, dst, local_sem.at[i])
        for i, (src, dst) in enumerate(
            [(low_in_hbm, lin), (panels_hbm, pan.at[z]), (low_out_hbm, lout), (cot_hbm, cot)]
        )
    ]
    feature_blocks, toks = tok.shape[:2]

    def token_copy(b):
        return pltpu.make_async_copy(
            tokens_hbm.at[:, pl.ds(pl.multiple_of(b * blk, blk), blk)], tok.at[b], tok_sem.at[b])

    def token_start(b, carry):
        token_copy(b).start()
        return carry

    def token_wait(b, carry):
        token_copy(b).wait()
        return carry

    in_copies[0].start()
    lax.fori_loop(0, feature_blocks, token_start, 0)
    for copy in in_copies[1:]:
        copy.start()

    barrier = pltpu.get_barrier_semaphore()

    @pl.when(z > 0)
    def _():
        pl.semaphore_signal(barrier, inc=1, device_id={"fsdp": z - 1}, device_id_type=MESH)

    @pl.when(z < nz - 1)
    def _():
        pl.semaphore_signal(barrier, inc=1, device_id={"fsdp": z + 1}, device_id_type=MESH)

    for i in range(1, nt):
        pl.semaphore_signal(
            barrier, inc=1, device_id={"tensor": lax.rem(t + i, nt)}, device_id_type=MESH)
    for i in range(1, ny):
        pl.semaphore_signal(
            barrier, inc=1, device_id={"dp": lax.rem(y + i, ny)}, device_id_type=MESH)
    neighbours = jnp.where(z > 0, 1, 0) + jnp.where(z < nz - 1, 1, 0)
    pl.semaphore_wait(barrier, nt - 1 + ny - 1 + neighbours)

    def span(j):
        return pl.ds(j * nc, nc)

    def gather_copy(way, shard, j, own_part):
        there = z + 1 if way == 0 else z - 1
        src = panels_hbm.at[span(j)] if own_part else pan.at[shard, span(j)]
        return pltpu.make_async_remote_copy(
            src_ref=src, dst_ref=pan.at[shard, span(j)],
            send_sem=ag_send.at[way, shard, j], recv_sem=ag_recv.at[shard, j],
            device_id={"fsdp": there}, device_id_type=MESH)

    def send_own(j):
        @pl.when(z < nz - 1)
        def _():
            gather_copy(0, z, j, True).start()

        @pl.when(z > 0)
        def _():
            gather_copy(1, z, j, True).start()

    def inside(j):
        return jnp.logical_and(j >= 0, j < chunks)

    def pass_on(h, tau):
        j = tau - (h - 1)
        ok = inside(j)

        @pl.when(jnp.logical_and(ok, z - h >= 0))
        def _():
            gather_copy(0, z - h, j, False).wait_recv()

            @pl.when(z < nz - 1)
            def _():
                gather_copy(0, z - h, j, False).start()

        @pl.when(jnp.logical_and(ok, z + h < nz))
        def _():
            gather_copy(1, z + h, j, False).wait_recv()

            @pl.when(z > 0)
            def _():
                gather_copy(1, z + h, j, False).start()

    for j in range(min(AHEAD, chunks)):
        send_own(j)

    in_copies[0].wait()
    lax.fori_loop(0, feature_blocks, token_wait, 0)
    blocks = lin.shape[0] // blk
    lpart[...] = jnp.dot(
        jnp.concatenate([tok[t * blocks + b] for b in range(blocks)], axis=1), lin[...],
        preferred_element_type=f32,
    ).reshape(lpart.shape)

    def lat_one(i):
        peer = lax.rem(t + i, nt)
        return pltpu.make_async_remote_copy(
            src_ref=lpart.at[peer], dst_ref=lrecv.at[i],
            send_sem=l1_send.at[i], recv_sem=l1_recv.at[i],
            device_id={"tensor": peer}, device_id_type=MESH)

    def lat_two(i, shard):
        peer = lax.rem(t + i, nt)
        return pltpu.make_async_remote_copy(
            src_ref=lat.at[shard], dst_ref=lat.at[shard],
            send_sem=l2_send.at[i], recv_sem=l2_recv.at[i],
            device_id={"tensor": peer}, device_id_type=MESH)

    for i in range(1, nt):
        lat_one(i).start()
    total = lpart[t]
    for i in range(1, nt):
        lat_one(i).wait_recv()
        total = total + lrecv[i]
    lat[t] = total.astype(lat.dtype)
    for i in range(1, nt):
        lat_two(i, t).start()
    for copy in in_copies[1:]:
        copy.wait()
    for i in range(1, nt):
        lat_two(i, lax.rem(t + nt - i, nt)).wait_recv()

    def column(c):
        picked = jnp.concatenate(
            [tok[rows_ref[c, k]] for k in range(per)], axis=1)
        weight = jnp.concatenate(
            [pan[s, c, k] for k in range(per) for s in range(nz)], axis=0)
        latent = lat[...].reshape(toks, -1)
        pre = jnp.dot(latent, lout[c], preferred_element_type=f32)
        pre = pre + jnp.dot(picked, weight, preferred_element_type=f32)
        at = pl.ds(pl.multiple_of(c * blk, blk), blk)
        square = pre * pre
        curve = jnp.tanh(GELU_SCALE * (pre + GELU_CUBIC * (square * pre)))
        half = 0.5 * (1.0 + curve)
        act_ref[:, at] = (pre * half).astype(act_ref.dtype)
        inner = GELU_SCALE * (1.0 + 3.0 * GELU_CUBIC * square)
        deriv = half + 0.5 * pre * (1.0 - curve * curve) * inner
        slope = (cot[:, at].astype(f32) * deriv).astype(jnp.bfloat16)
        grad = lax.dot_general(
            picked, slope, (((0,), (0,)), ((), ())), preferred_element_type=f32)
        own[c] = grad.reshape(per, blk, blk)

    def sum_copy(way, d, j):
        there = z + 1 if way == 0 else z - 1
        return pltpu.make_async_remote_copy(
            src_ref=sbuf.at[d, span(j)], dst_ref=rbuf.at[way, d, span(j)],
            send_sem=rs_send.at[d, j], recv_sem=rs_recv.at[way, d, j],
            device_id={"fsdp": there}, device_id_type=MESH)

    def own_part(d, j):
        return own[span(j), :, pl.ds(pl.multiple_of(d * rows, rows), rows), :]

    def flow(way, d, j, first):
        @pl.when(first)
        def _():
            sbuf[d, span(j)] = own_part(d, j).astype(sbuf.dtype)

        @pl.when(jnp.logical_not(first))
        def _():
            sum_copy(way, d, j).wait_recv()
            sbuf[d, span(j)] = (
                own_part(d, j) + rbuf[way, d, span(j)].astype(f32)).astype(sbuf.dtype)

        sum_copy(way, d, j).start()

    def dp_copy(i, j):
        peer = lax.rem(y + i, ny)
        return pltpu.make_async_remote_copy(
            src_ref=ysend.at[span(j)], dst_ref=yrecv.at[y, span(j)],
            send_sem=y_send.at[i, j], recv_sem=y_recv.at[i, j],
            device_id={"dp": peer}, device_id_type=MESH)

    def step(tau, carry):
        @pl.when(tau + AHEAD < chunks)
        def _():
            send_own(tau + AHEAD)

        def hop(h, carry):
            pass_on(h, tau)
            return carry

        lax.fori_loop(1, nz, hop, 0)

        now = tau - (nz - 2)

        @pl.when(inside(now))
        def _():
            for i in range(nc):
                column(now * nc + i)

        up, down = now - z, now - (nz - 1 - z)

        def towards(d, carry):
            @pl.when(jnp.logical_and(d > z, inside(up)))
            def _():
                flow(0, d, up, z == 0)

            @pl.when(jnp.logical_and(d < z, inside(down)))
            def _():
                flow(1, d, down, z == nz - 1)

            return carry

        lax.fori_loop(0, nz, towards, 0)

        last = now - (nz - 1)

        @pl.when(inside(last))
        def _():
            ysend[span(last)] = own_part(z, last)

            @pl.when(z > 0)
            def _():
                sum_copy(0, z, last).wait_recv()
                ysend[span(last)] += rbuf[0, z, span(last)].astype(f32)

            @pl.when(z < nz - 1)
            def _():
                sum_copy(1, z, last).wait_recv()
                ysend[span(last)] += rbuf[1, z, span(last)].astype(f32)

            for i in range(1, ny):
                dp_copy(i, last).start()
            yrecv[y, span(last)] = ysend[span(last)]

        done = now - nz

        @pl.when(inside(done))
        def _():
            for i in range(1, ny):
                dp_copy(i, done).wait_recv()
            value = yrecv[0, span(done)]
            for i in range(1, ny):
                value = value + yrecv[i, span(done)]
            grad_ref[span(done)] = value

        return carry

    lax.fori_loop(0, chunks + (nz - 2) + nz, step, 0)

    for i in range(1, nt):
        lat_one(i).wait_send()
        lat_two(i, t).wait_send()

    def drain(j, carry):
        for i in range(1, ny):
            dp_copy(i, j).wait_send()

        def each(s, carry):
            @pl.when(jnp.logical_and(s <= z, z < nz - 1))
            def _():
                gather_copy(0, s, j, False).wait_send()

            @pl.when(jnp.logical_and(s >= z, z > 0))
            def _():
                gather_copy(1, s, j, False).wait_send()

            @pl.when(s > z)
            def _():
                sum_copy(0, s, j).wait_send()

            @pl.when(s < z)
            def _():
                sum_copy(1, s, j).wait_send()

            return carry

        return lax.fori_loop(0, nz, each, carry)

    lax.fori_loop(0, chunks, drain, 0)


def on_device(sizes, tokens, panels, block_rows, low_in, low_out, cotangent):
    nz, ny, nt = sizes
    cols, per, rows, blk = panels.shape
    toks, rank = tokens.shape[0], low_in.shape[1]
    nc = 2 if cols % 2 == 0 else 1
    chunks = cols // nc
    bf16, f32 = jnp.bfloat16, jnp.float32
    hop_type = bf16 if nz <= 4 else f32
    low_out = low_out.reshape(cols, rank, blk)
    hbm = pl.BlockSpec(memory_space=pl.ANY)
    vmem = pl.BlockSpec(memory_space=pltpu.VMEM)
    dma = pltpu.SemaphoreType.DMA
    return pl.pallas_call(
        functools.partial(kernel, nz, ny, nt, nc),
        out_shape=(
            jax.ShapeDtypeStruct(cotangent.shape, bf16),
            jax.ShapeDtypeStruct(panels.shape, f32),
        ),
        in_specs=[hbm, hbm, pl.BlockSpec(memory_space=pltpu.SMEM), hbm, hbm, hbm],
        out_specs=(vmem, vmem),
        scratch_shapes=[
            pltpu.VMEM((tokens.shape[1] // blk, toks, blk), bf16),
            pltpu.VMEM(low_in.shape, bf16),
            pltpu.VMEM(low_out.shape, bf16),
            pltpu.VMEM(cotangent.shape, bf16),
            pltpu.VMEM((nz,) + panels.shape, bf16),
            pltpu.VMEM((cols, per, blk, blk), f32),
            pltpu.VMEM((nz,) + panels.shape, hop_type),
            pltpu.VMEM((2, nz) + panels.shape, hop_type),
            pltpu.VMEM(panels.shape, f32),
            pltpu.VMEM((ny,) + panels.shape, f32),
            pltpu.VMEM((nt, toks // nt, rank), f32),
            pltpu.VMEM((nt, toks // nt, rank), f32),
            pltpu.VMEM((nt, toks // nt, rank), bf16),
            dma((4,)),
            dma((tokens.shape[1] // blk,)),
            dma((2, nz, chunks)),
            dma((nz, chunks)),
            dma((nz, chunks)),
            dma((2, nz, chunks)),
            dma((ny, chunks)),
            dma((ny, chunks)),
            dma((nt,)),
            dma((nt,)),
            dma((nt,)),
            dma((nt,)),
        ],
        compiler_params=pltpu.CompilerParams(
            collective_id=0, has_side_effects=True, vmem_limit_bytes=60 * 1024 * 1024),
    )(tokens, panels, block_rows, low_in, low_out, cotangent)


def solution(mesh):
    in_specs = (
        P(("fsdp", "dp"), None),
        P("tensor", None, "fsdp", None),
        P("tensor", None),
        P("tensor", None),
        P("tensor", None, None, None),
        P(("fsdp", "dp"), "tensor"),
    )
    out_specs = (P(("fsdp", "dp"), "tensor"), P("tensor", None, "fsdp", None))
    sizes = tuple(mesh.shape[name] for name in ("fsdp", "dp", "tensor"))
    return jax.shard_map(
        functools.partial(on_device, sizes),
        mesh=mesh, in_specs=in_specs, out_specs=out_specs, check_vma=False,
    )
```

time: 303 us -> 123 us (0.41)
  waiting for transfers between devices: 204 us -> 0 us
  Pallas kernels: 0 us -> 117 us
  local copies, waits for them, and re-layouts: 42 us -> 5.58 us
  matrix products: 23.5 us -> 0 us
  blocking collectives: 19.1 us -> 0 us
  between operations: 13.8 us -> 0.65 us
    reduce_scatter x1 -> x0, waiting for transfers between devices: 126 us -> none  [on_device(): lax.psum_scatter(local_grad, 'fsdp', scatter_dimension=2, tiled=True)]
    pallas_call x0 -> x1, Pallas kernels: none -> 117 us  [on_device(): pl.pallas_call(functools.partial(kernel, nz, ny, nt, nc), out_shape=(jax....]
    psum x1 -> x0, waiting for transfers between devices: 56.2 us -> none  [on_device(): panel_grad = lax.psum(grad_shard, 'dp')]
    dot_general x4 -> x0, matrix products: 23.5 us -> none  [the longest x1 8.1 us: on_device(): jnp.einsum('tckr,tco->ckro', picked, slope, preferred_element_type=jnp.fl...]
    all_gather x1 -> x0, waiting for transfers between devices: 20.3 us -> none  [on_device(): panels_all = lax.all_gather(panels, 'fsdp', axis=2, tiled=True)]
    psum x1 -> x0, blocking collectives: 19.1 us -> none  [on_device(): latent = lax.psum(partial_low, 'tensor').astype(jnp.bfloat16)]
    gather x2 -> x0, local copies, waits for them, and re-layouts: 19.1 us -> none  [on_device(): picked = jnp.take(tiled_rows, block_rows.reshape(-1), axis=1)]
    unnamed x12 -> x5, local copies, waits for them, and re-layouts: 12.8 us -> 5.58 us
  transfers between devices with their start and end apart: 3 -> 0, of which waited for: 3 -> 0; matrix products, arithmetic and copies ran while one was open for 14% -> 0% of each run, Pallas kernels for 0% -> 0%
where the time goes in v1:
time: 123 us
  Pallas kernels  117 us (95%)
  local copies, waits for them, and re-layouts  5.58 us (5%)
    pallas_call x1, Pallas kernels, on_device(): pl.pallas_call(functools.partial(kernel, nz, ny, nt, nc), out_shape=(jax....  117 us
    unnamed x5, local copies, waits for them, and re-layouts  5.58 us

profile of v1, /device:TPU:0, one launch (start us, length us, event | category | flops | bytes accessed | tf_op | source)
XLA Modules:
  0.0 122.9 jit_solution(8313610688873383076)
XLA Ops:
  0.6 1.4 %copy.8.rows_ref = s32[28,4]{1,0:T(8,128)} copy(s32[28,4]{0,1:T(4,128)} %param.8) | data formatting | bytes 896 | tf_op args[2]
  2.0 116.7 %shard_map.77 = (bf16[256,3584]{1,0:T(8,128)(2,1)}, f32[28,4,32,128]{3,2,1,0:T(8,128)}) custom-call(bf16[256,7168]{1,0:T(8,128)(2,1)} %tokens_hbm.1, bf16[28,4,32,128]{3,2,1,0:T(8,128)(2,1)} %panels_hbm.1, s32[28,4]{1,0:T(8,128)} %copy.8.rows_ref, bf16[1792,512]{1,0:T(8,128)(2,1)} %low_in_hbm.1, bf16[28,512,128]{2,1,0:T(8,128)(2,1)} %bitcast.1, ...), custom_call_target="tpu_custom_call" | custom-call | tf_op jit(solution)/shard_map/pallas_call | solution.py:318
  118.7 0.0 copy-start
  118.7 3.0 %copy.11 = bf16[256,3584]{1,0:T(8,128)(2,1)} copy(bf16[256,3584]{1,0:T(8,128)(2,1)} %get-tuple-element.4) | data formatting | bytes 3670016
  121.7 0.0 copy-done
  121.7 1.2 copy.12
Async XLA Ops:
  118.7 3.0 %copy-start = (f32[28,4,32,128]{3,2,1,0:T(8,128)S(1)}, f32[28,4,32,128]{3,2,1,0:T(8,128)}, u32[]{:S(2)}) copy-start(f32[28,4,32,128]{3,2,1,0:T(8,128)} %get-tuple-element.5) | copy-start | bytes 5505028

commit v2 on v1

v2 whole, which is shorter than its diff:
```python
import functools
import math

import jax
import jax.numpy as jnp
from jax import lax
from jax.experimental import pallas as pl
from jax.experimental.pallas import tpu as pltpu
from jax.sharding import PartitionSpec as P

MESH = pl.DeviceIdType.MESH
GELU_SCALE = math.sqrt(2.0 / math.pi)
GELU_CUBIC = 0.044715
AHEAD = 2
SPLIT = (1, 1)
EARLY = (1, 2)


def chosen(pattern, j):
    count, period = pattern
    return lax.rem(j * count, period) < count


def either(pattern, j, act):
    if pattern[0] == pattern[1]:
        act(True)
    elif pattern[0] == 0:
        act(False)
    else:
        pl.when(chosen(pattern, j))(lambda: act(True))
        pl.when(jnp.logical_not(chosen(pattern, j)))(lambda: act(False))


def kernel(
    nz, ny, nt, per,
    tokens_hbm, panels_hbm, rows_hbm, low_in_hbm, low_out_hbm, cot_hbm,
    act_ref, grad_ref,
    rows_ref, tok, lin, lout, cot, pan, own, sbuf, rbuf, ysend, yrecv, xsend, xrecv,
    lpart, lrecv, lat,
    local_sem, tok_sem, ag_send, ag_recv, ay_send, ay_recv, rs_send, rs_recv,
    y_send, y_recv, x_send, x_recv, l1_send, l1_recv, l2_send, l2_recv,
):
    z, y, t = lax.axis_index("fsdp"), lax.axis_index("dp"), lax.axis_index("tensor")
    cells, rows, blk = panels_hbm.shape
    chunks = ag_recv.shape[1]
    size = cells // chunks
    part = size // ny
    nc = size // per
    f32 = jnp.float32

    in_copies = [
        pltpu.make_async_copy(src, dst, local_sem.at[i])
        for i, (src, dst) in enumerate(
            [(low_in_hbm, lin), (panels_hbm, pan.at[z]), (low_out_hbm, lout), (cot_hbm, cot),
             (rows_hbm, rows_ref)]
        )
    ]
    feature_blocks, toks = tok.shape[:2]

    def token_copy(b):
        return pltpu.make_async_copy(
            tokens_hbm.at[:, pl.ds(pl.multiple_of(b * blk, blk), blk)], tok.at[b], tok_sem.at[b])

    def token_start(b, carry):
        token_copy(b).start()
        return carry

    def token_wait(b, carry):
        token_copy(b).wait()
        return carry

    in_copies[0].start()
    lax.fori_loop(0, feature_blocks, token_start, 0)
    for copy in in_copies[1:]:
        copy.start()

    barrier = pltpu.get_barrier_semaphore()

    @pl.when(z > 0)
    def _():
        pl.semaphore_signal(barrier, inc=1, device_id={"fsdp": z - 1}, device_id_type=MESH)

    @pl.when(z < nz - 1)
    def _():
        pl.semaphore_signal(barrier, inc=1, device_id={"fsdp": z + 1}, device_id_type=MESH)

    for i in range(1, nt):
        pl.semaphore_signal(
            barrier, inc=1, device_id={"tensor": lax.rem(t + i, nt)}, device_id_type=MESH)
    for i in range(1, ny):
        pl.semaphore_signal(
            barrier, inc=1, device_id={"dp": lax.rem(y + i, ny)}, device_id_type=MESH)
    neighbours = jnp.where(z > 0, 1, 0) + jnp.where(z < nz - 1, 1, 0)
    pl.semaphore_wait(barrier, nt - 1 + ny - 1 + neighbours)

    def span(j, p=None):
        if p is None:
            return pl.ds(j * size, size)
        return pl.ds(j * size + p * part, part)

    def mine(cut):
        return y if cut else None

    def gather_copy(way, shard, j, cut, from_input=False):
        there = z + 1 if way == 0 else z - 1
        at = span(j, mine(cut))
        src = panels_hbm.at[at] if from_input else pan.at[shard, at]
        return pltpu.make_async_remote_copy(
            src_ref=src, dst_ref=pan.at[shard, at],
            send_sem=ag_send.at[way, shard, j], recv_sem=ag_recv.at[shard, j],
            device_id={"fsdp": there}, device_id_type=MESH)

    def across_copy(i, shard, j, p):
        at = span(j, p)
        return pltpu.make_async_remote_copy(
            src_ref=pan.at[shard, at], dst_ref=pan.at[shard, at],
            send_sem=ay_send.at[i, shard, j], recv_sem=ay_recv.at[i, shard, j],
            device_id={"dp": lax.rem(y + i, ny)}, device_id_type=MESH)

    def send_own(j):
        def act(cut):
            @pl.when(z < nz - 1)
            def _():
                gather_copy(0, z, j, cut, True).start()

            @pl.when(z > 0)
            def _():
                gather_copy(1, z, j, cut, True).start()

        either(SPLIT, j, act)

    def inside(j):
        return jnp.logical_and(j >= 0, j < chunks)

    def pass_on(h, tau):
        j = tau - (h - 1)
        ok = inside(j)

        def arrived(way, shard, more):
            def act(cut):
                gather_copy(way, shard, j, cut).wait_recv()

                @pl.when(more)
                def _():
                    gather_copy(way, shard, j, cut).start()

                if cut:
                    for i in range(1, ny):
                        across_copy(i, shard, j, y).start()

            either(SPLIT, j, act)

        @pl.when(jnp.logical_and(ok, z - h >= 0))
        def _():
            arrived(0, z - h, z < nz - 1)

        @pl.when(jnp.logical_and(ok, z + h < nz))
        def _():
            arrived(1, z + h, z > 0)

    for j in range(min(AHEAD, chunks)):
        send_own(jnp.int32(j))

    in_copies[0].wait()
    lax.fori_loop(0, feature_blocks, token_wait, 0)
    blocks = lin.shape[0] // blk
    lpart[...] = jnp.dot(
        jnp.concatenate([tok[t * blocks + b] for b in range(blocks)], axis=1), lin[...],
        preferred_element_type=f32,
    ).reshape(lpart.shape)

    def lat_one(i):
        peer = lax.rem(t + i, nt)
        return pltpu.make_async_remote_copy(
            src_ref=lpart.at[peer], dst_ref=lrecv.at[i],
            send_sem=l1_send.at[i], recv_sem=l1_recv.at[i],
            device_id={"tensor": peer}, device_id_type=MESH)

    def lat_two(i, shard):
        peer = lax.rem(t + i, nt)
        return pltpu.make_async_remote_copy(
            src_ref=lat.at[shard], dst_ref=lat.at[shard],
            send_sem=l2_send.at[i], recv_sem=l2_recv.at[i],
            device_id={"tensor": peer}, device_id_type=MESH)

    for i in range(1, nt):
        lat_one(i).start()

    def latent_sum():
        total = lpart[t]
        for i in range(1, nt):
            lat_one(i).wait_recv()
            total = total + lrecv[i]
        lat[t] = total.astype(lat.dtype)
        for i in range(1, nt):
            lat_two(i, t).start()
        for copy in in_copies[1:]:
            copy.wait()

    def latent_done():
        for i in range(1, nt):
            lat_two(i, lax.rem(t + nt - i, nt)).wait_recv()

    def column(c):
        picked = jnp.concatenate([tok[rows_ref[c, k]] for k in range(per)], axis=1)
        weight = jnp.concatenate(
            [pan[s, c * per + k] for k in range(per) for s in range(nz)], axis=0)
        latent = lat[...].reshape(toks, -1)
        pre = jnp.dot(latent, lout[c], preferred_element_type=f32)
        pre = pre + jnp.dot(picked, weight, preferred_element_type=f32)
        at = pl.ds(pl.multiple_of(c * blk, blk), blk)
        square = pre * pre
        curve = jnp.tanh(GELU_SCALE * (pre + GELU_CUBIC * (square * pre)))
        half = 0.5 * (1.0 + curve)
        act_ref[:, at] = (pre * half).astype(act_ref.dtype)
        inner = GELU_SCALE * (1.0 + 3.0 * GELU_CUBIC * square)
        deriv = half + 0.5 * pre * (1.0 - curve * curve) * inner
        slope = (cot[:, at].astype(f32) * deriv).astype(jnp.bfloat16)
        grad = lax.dot_general(
            picked, slope, (((0,), (0,)), ((), ())), preferred_element_type=f32)
        own[pl.ds(c * per, per)] = grad.reshape(per, blk, blk)

    def sum_copy(way, d, j, cut):
        there = z + 1 if way == 0 else z - 1
        at = span(j, mine(cut))
        return pltpu.make_async_remote_copy(
            src_ref=sbuf.at[d, at], dst_ref=rbuf.at[way, d, at],
            send_sem=rs_send.at[d, j], recv_sem=rs_recv.at[way, d, j],
            device_id={"fsdp": there}, device_id_type=MESH)

    def own_part(d, at):
        return own[at, pl.ds(pl.multiple_of(d * rows, rows), rows), :]

    def flow(way, d, j, first):
        def act(cut):
            at = span(j, mine(cut))

            @pl.when(first)
            def _():
                sbuf[d, at] = own_part(d, at).astype(sbuf.dtype)

            @pl.when(jnp.logical_not(first))
            def _():
                sum_copy(way, d, j, cut).wait_recv()
                sbuf[d, at] = (own_part(d, at) + rbuf[way, d, at].astype(f32)).astype(sbuf.dtype)

            sum_copy(way, d, j, cut).start()

        either(EARLY, j, act)

    def early_copy(i, j):
        peer = lax.rem(y + i, ny)
        return pltpu.make_async_remote_copy(
            src_ref=xsend.at[span(j, peer)], dst_ref=xrecv.at[y, pl.ds(j * part, part)],
            send_sem=x_send.at[i, j], recv_sem=x_recv.at[i, j],
            device_id={"dp": peer}, device_id_type=MESH)

    def early_start(j):
        def act(cut):
            if cut:
                for i in range(1, ny):
                    at = span(j, lax.rem(y + i, ny))
                    xsend[at] = own[at].astype(xsend.dtype)
                    early_copy(i, j).start()

        either(EARLY, j, act)

    def early_done(j):
        def act(cut):
            if cut:
                total = own[span(j, y)]
                for i in range(1, ny):
                    early_copy(i, j).wait_recv()
                    total = total + xrecv[lax.rem(y + i, ny), pl.ds(j * part, part)].astype(f32)
                own[span(j, y)] = total

        either(EARLY, j, act)

    def dp_copy(i, j, cut):
        at = span(j, mine(cut))
        return pltpu.make_async_remote_copy(
            src_ref=ysend.at[at], dst_ref=yrecv.at[y, at],
            send_sem=y_send.at[i, j], recv_sem=y_recv.at[i, j],
            device_id={"dp": lax.rem(y + i, ny)}, device_id_type=MESH)

    def finish(j):
        def act(cut):
            at = span(j, mine(cut))

            def landed(way):
                sum_copy(way, z, j, cut).wait_recv()
                return rbuf[way, z, at].astype(f32)

            @pl.when(z == 0)
            def _():
                ysend[at] = (own_part(z, at) + landed(1)).astype(ysend.dtype)

            @pl.when(z == nz - 1)
            def _():
                ysend[at] = (own_part(z, at) + landed(0)).astype(ysend.dtype)

            @pl.when(jnp.logical_and(z > 0, z < nz - 1))
            def _():
                ysend[at] = (own_part(z, at) + landed(0) + landed(1)).astype(ysend.dtype)

            for i in range(1, ny):
                dp_copy(i, j, cut).start()
            yrecv[y, at] = ysend[at]

        either(EARLY, j, act)

    def result(j):
        def act(cut):
            for i in range(1, ny):
                dp_copy(i, j, cut).wait_recv()
            if cut:
                for p in range(ny):
                    grad_ref[span(j, p)] = yrecv[p, span(j, p)].astype(f32)
            else:
                value = yrecv[0, span(j)].astype(f32)
                for p in range(1, ny):
                    value = value + yrecv[p, span(j)].astype(f32)
                grad_ref[span(j)] = value

        either(EARLY, j, act)

    def across_done(j):
        def act(cut):
            if cut:
                for i in range(1, ny):
                    def each(s, carry):
                        @pl.when(s != z)
                        def _():
                            across_copy(i, s, j, lax.rem(y + ny - i, ny)).wait_recv()

                        return carry

                    lax.fori_loop(0, nz, each, 0)

        either(SPLIT, j, act)

    def step(tau, carry):
        @pl.when(tau + AHEAD < chunks)
        def _():
            send_own(tau + AHEAD)

        def hop(h, carry):
            pass_on(h, tau)
            return carry

        lax.fori_loop(1, nz, hop, 0)

        pl.when(tau == 0)(latent_sum)
        pl.when(tau == 1)(latent_done)
        now = tau - (nz - 1)

        @pl.when(inside(now))
        def _():
            across_done(now)
            for i in range(nc):
                column(now * nc + i)
            early_start(now)

        summed = now - 1 if EARLY[0] else now
        if EARLY[0]:
            pl.when(inside(summed))(lambda: early_done(summed))
        up, down = summed - z, summed - (nz - 1 - z)

        def towards(d, carry):
            @pl.when(jnp.logical_and(d > z, inside(up)))
            def _():
                flow(0, d, up, z == 0)

            @pl.when(jnp.logical_and(d < z, inside(down)))
            def _():
                flow(1, d, down, z == nz - 1)

            return carry

        lax.fori_loop(0, nz, towards, 0)
        last = summed - (nz - 1)
        pl.when(inside(last))(lambda: finish(last))
        done = last - 1
        pl.when(inside(done))(lambda: result(done))
        return carry

    lax.fori_loop(0, chunks + 2 * nz - 1 + (1 if EARLY[0] else 0), step, 0)

    for i in range(1, nt):
        lat_one(i).wait_send()
        lat_two(i, t).wait_send()

    def drain(j, carry):
        def panels_left(cut):
            def each(s, carry):
                @pl.when(jnp.logical_and(s <= z, z < nz - 1))
                def _():
                    gather_copy(0, s, j, cut).wait_send()

                @pl.when(jnp.logical_and(s >= z, z > 0))
                def _():
                    gather_copy(1, s, j, cut).wait_send()

                if cut:
                    @pl.when(s != z)
                    def _():
                        for i in range(1, ny):
                            across_copy(i, s, j, y).wait_send()

                return carry

            lax.fori_loop(0, nz, each, 0)

        def sums_left(cut):
            def each(s, carry):
                @pl.when(s > z)
                def _():
                    sum_copy(0, s, j, cut).wait_send()

                @pl.when(s < z)
                def _():
                    sum_copy(1, s, j, cut).wait_send()

                return carry

            lax.fori_loop(0, nz, each, 0)
            for i in range(1, ny):
                dp_copy(i, j, cut).wait_send()
                if cut:
                    early_copy(i, j).wait_send()

        either(SPLIT, j, panels_left)
        either(EARLY, j, sums_left)
        return carry

    lax.fori_loop(0, chunks, drain, 0)


def on_device(sizes, tokens, panels, block_rows, low_in, low_out, cotangent):
    nz, ny, nt = sizes
    cols, per, rows, blk = panels.shape
    toks, rank = tokens.shape[0], low_in.shape[1]
    nc = 4 if cols % 4 == 0 else 2 if cols % 2 == 0 else 1
    chunks = cols // nc
    bf16, f32 = jnp.bfloat16, jnp.float32
    hop_type = bf16 if nz <= 4 and ny <= 2 else f32
    low_out = low_out.reshape(cols, rank, blk)
    cells = panels.reshape(cols * per, rows, blk)
    hbm = pl.BlockSpec(memory_space=pl.ANY)
    vmem = pl.BlockSpec(memory_space=pltpu.VMEM)
    dma = pltpu.SemaphoreType.DMA
    early_cells = cells.shape[0] if EARLY[0] else chunks * ny
    early_tile = (blk, blk) if EARLY[0] else (8, blk)
    activated, grad = pl.pallas_call(
        functools.partial(kernel, nz, ny, nt, per),
        out_shape=(
            jax.ShapeDtypeStruct(cotangent.shape, bf16),
            jax.ShapeDtypeStruct(cells.shape, f32),
        ),
        in_specs=[hbm] * 6,
        out_specs=(vmem, vmem),
        scratch_shapes=[
            pltpu.SMEM(block_rows.shape, jnp.int32),
            pltpu.VMEM((tokens.shape[1] // blk, toks, blk), bf16),
            pltpu.VMEM(low_in.shape, bf16),
            pltpu.VMEM(low_out.shape, bf16),
            pltpu.VMEM(cotangent.shape, bf16),
            pltpu.VMEM((nz,) + cells.shape, bf16),
            pltpu.VMEM((cols * per, blk, blk), f32),
            pltpu.VMEM((nz,) + cells.shape, hop_type),
            pltpu.VMEM((2, nz) + cells.shape, hop_type),
            pltpu.VMEM(cells.shape, hop_type),
            pltpu.VMEM((ny,) + cells.shape, hop_type),
            pltpu.VMEM((early_cells,) + early_tile, hop_type),
            pltpu.VMEM((ny, early_cells // ny) + early_tile, hop_type),
            pltpu.VMEM((nt, toks // nt, rank), f32),
            pltpu.VMEM((nt, toks // nt, rank), f32),
            pltpu.VMEM((nt, toks // nt, rank), bf16),
            dma((5,)),
            dma((tokens.shape[1] // blk,)),
            dma((2, nz, chunks)),
            dma((nz, chunks)),
            dma((ny, nz, chunks)),
            dma((ny, nz, chunks)),
            dma((nz, chunks)),
            dma((2, nz, chunks)),
            dma((ny, chunks)),
            dma((ny, chunks)),
            dma((ny, chunks)),
            dma((ny, chunks)),
            dma((nt,)),
            dma((nt,)),
            dma((nt,)),
            dma((nt,)),
        ],
        compiler_params=pltpu.CompilerParams(
            collective_id=0, has_side_effects=True, vmem_limit_bytes=60 * 1024 * 1024),
    )(tokens, cells, block_rows, low_in, low_out, cotangent)
    return activated, grad.reshape(panels.shape)


def solution(mesh):
    in_specs = (
        P(("fsdp", "dp"), None),
        P("tensor", None, "fsdp", None),
        P("tensor", None),
        P("tensor", None),
        P("tensor", None, None, None),
        P(("fsdp", "dp"), "tensor"),
    )
    out_specs = (P(("fsdp", "dp"), "tensor"), P("tensor", None, "fsdp", None))
    sizes = tuple(mesh.shape[name] for name in ("fsdp", "dp", "tensor"))
    return jax.shard_map(
        functools.partial(on_device, sizes),
        mesh=mesh, in_specs=in_specs, out_specs=out_specs, check_vma=False,
    )
```

time: 123 us -> 101 us (0.82)
  Pallas kernels: 117 us -> 94.8 us
    pallas_call x1, Pallas kernels: 117 us -> 94.8 us  [on_device(): pl.pallas_call(functools.partial(kernel, nz, ny, nt, per), out_shape=(jax...]
where the time goes in v2:
time: 101 us
  Pallas kernels  94.8 us (94%)
  local copies, waits for them, and re-layouts  5.58 us (6%)
    pallas_call x1, Pallas kernels, on_device(): pl.pallas_call(functools.partial(kernel, nz, ny, nt, per), out_shape=(jax...  94.8 us
    unnamed x5, local copies, waits for them, and re-layouts  5.58 us

profile of v2, /device:TPU:0, one launch (start us, length us, event | category | flops | bytes accessed | tf_op | source)
XLA Modules:
  0.0 101.0 jit_solution(127929401316045534)
XLA Ops:
  0.6 1.4 %copy.8.rows_hbm = s32[28,4]{1,0:T(8,128)} copy(s32[28,4]{0,1:T(4,128)} %param.8) | data formatting | bytes 896 | tf_op args[2]
  2.0 94.8 %shard_map.77 = (bf16[256,3584]{1,0:T(8,128)(2,1)}, f32[112,32,128]{2,1,0:T(8,128)}) custom-call(bf16[256,7168]{1,0:T(8,128)(2,1)} %tokens_hbm.1, bf16[112,32,128]{2,1,0:T(8,128)(2,1)} %bitcast.5, s32[28,4]{1,0:T(8,128)} %copy.8.rows_hbm, bf16[1792,512]{1,0:T(8,128)(2,1)} %low_in_hbm.1, bf16[28,512,128]{2,1,0:T(8,128)(2,1)} %bitcast.3, bf16[256,3584]{1,0:T(8,128)(2,1)} %cot_hbm.1), custom_call_target="tpu_custom_call" | custom-call | tf_op jit(solution)/shard_map/pallas_call | solution.py:454
  96.8 0.0 copy-start
  96.8 3.0 %copy.11 = bf16[256,3584]{1,0:T(8,128)(2,1)} copy(bf16[256,3584]{1,0:T(8,128)(2,1)} %get-tuple-element.8) | data formatting | bytes 3670016
  99.8 0.0 copy-done
  99.8 1.2 %copy.12 = f32[28,4,32,128]{3,2,1,0:T(8,128)} copy(f32[28,4,32,128]{3,2,1,0:T(8,128)S(1)} %bitcast.4) | data formatting | bytes 3670016
Async XLA Ops:
  96.8 3.0 %copy-start = (f32[112,32,128]{2,1,0:T(8,128)S(1)}, f32[112,32,128]{2,1,0:T(8,128)}, u32[]{:S(2)}) copy-start(f32[112,32,128]{2,1,0:T(8,128)} %get-tuple-element.5) | copy-start | bytes 5505028

commit v3 on v2

--- a/solution.py
+++ b/solution.py
@@ -161,14 +161,6 @@
     for j in range(min(AHEAD, chunks)):
         send_own(jnp.int32(j))
 
-    in_copies[0].wait()
-    lax.fori_loop(0, feature_blocks, token_wait, 0)
-    blocks = lin.shape[0] // blk
-    lpart[...] = jnp.dot(
-        jnp.concatenate([tok[t * blocks + b] for b in range(blocks)], axis=1), lin[...],
-        preferred_element_type=f32,
-    ).reshape(lpart.shape)
-
     def lat_one(i):
         peer = lax.rem(t + i, nt)
         return pltpu.make_async_remote_copy(
@@ -183,8 +175,16 @@
             send_sem=l2_send.at[i], recv_sem=l2_recv.at[i],
             device_id={"tensor": peer}, device_id_type=MESH)
 
-    for i in range(1, nt):
-        lat_one(i).start()
+    def latent_part():
+        in_copies[0].wait()
+        lax.fori_loop(0, feature_blocks, token_wait, 0)
+        blocks = lin.shape[0] // blk
+        lpart[...] = jnp.dot(
+            jnp.concatenate([tok[t * blocks + b] for b in range(blocks)], axis=1), lin[...],
+            preferred_element_type=f32,
+        ).reshape(lpart.shape)
+        for i in range(1, nt):
+            lat_one(i).start()
 
     def latent_sum():
         total = lpart[t]
@@ -350,8 +350,9 @@
 
         lax.fori_loop(1, nz, hop, 0)
 
-        pl.when(tau == 0)(latent_sum)
-        pl.when(tau == 1)(latent_done)
+        pl.when(tau == 0)(latent_part)
+        pl.when(tau == 1)(latent_sum)
+        pl.when(tau == 2)(latent_done)
         now = tau - (nz - 1)
 
         @pl.when(inside(now))
@@ -367,9 +368,11 @@
         up, down = summed - z, summed - (nz - 1 - z)
 
         def towards(d, carry):
-            @pl.when(jnp.logical_and(d > z, inside(up)))
-            def _():
-                flow(0, d, up, z == 0)
+            far = nz - 1 - d
+
+            @pl.when(jnp.logical_and(far > z, inside(up)))
+            def _():
+                flow(0, far, up, z == 0)
 
             @pl.when(jnp.logical_and(d < z, inside(down)))
             def _():

time: 101 us -> 99.8 us (0.988)
  Pallas kernels: 94.8 us -> 93.4 us
    pallas_call x1, Pallas kernels: 94.8 us -> 93.4 us  [on_device(): pl.pallas_call(functools.partial(kernel, nz, ny, nt, per), out_shape=(jax...]
where the time goes in v3:
time: 99.8 us; the launch traced here: 99.6 us
  Pallas kernels  93.4 us (94%)
  local copies, waits for them, and re-layouts  5.58 us (6%)
    pallas_call x1, Pallas kernels, on_device(): pl.pallas_call(functools.partial(kernel, nz, ny, nt, per), out_shape=(jax...  93.4 us
    unnamed x5, local copies, waits for them, and re-layouts  5.58 us

profile of v3, /device:TPU:0, one launch (start us, length us, event | category | flops | bytes accessed | tf_op | source)
XLA Modules:
  0.0 99.6 jit_solution(9501551367496485115)
XLA Ops:
  0.6 1.4 %copy.8.rows_hbm = s32[28,4]{1,0:T(8,128)} copy(s32[28,4]{0,1:T(4,128)} %param.8) | data formatting | bytes 896 | tf_op args[2]
  2.0 93.4 %shard_map.77 = (bf16[256,3584]{1,0:T(8,128)(2,1)}, f32[112,32,128]{2,1,0:T(8,128)}) custom-call(bf16[256,7168]{1,0:T(8,128)(2,1)} %tokens_hbm.1, bf16[112,32,128]{2,1,0:T(8,128)(2,1)} %bitcast.5, s32[28,4]{1,0:T(8,128)} %copy.8.rows_hbm, bf16[1792,512]{1,0:T(8,128)(2,1)} %low_in_hbm.1, bf16[28,512,128]{2,1,0:T(8,128)(2,1)} %bitcast.3, bf16[256,3584]{1,0:T(8,128)(2,1)} %cot_hbm.1), custom_call_target="tpu_custom_call" | custom-call | tf_op jit(solution)/shard_map/pallas_call | solution.py:457
  95.4 0.0 copy-start
  95.4 3.0 %copy.11 = bf16[256,3584]{1,0:T(8,128)(2,1)} copy(bf16[256,3584]{1,0:T(8,128)(2,1)} %get-tuple-element.8) | data formatting | bytes 3670016
  98.4 0.0 copy-done
  98.4 1.2 %copy.12 = f32[28,4,32,128]{3,2,1,0:T(8,128)} copy(f32[28,4,32,128]{3,2,1,0:T(8,128)S(1)} %bitcast.4) | data formatting | bytes 3670016
Async XLA Ops:
  95.4 3.0 %copy-start = (f32[112,32,128]{2,1,0:T(8,128)S(1)}, f32[112,32,128]{2,1,0:T(8,128)}, u32[]{:S(2)}) copy-start(f32[112,32,128]{2,1,0:T(8,128)} %get-tuple-element.5) | copy-start | bytes 5505028
